TPU v7x, 32 devices: a whole 2x2x4 slice. The times are simulated.
32 devices in a mesh: node: 8 (over z, x), mp: 4 (over y, core).
Axes of the slice: x: 2, y: 2, z: 4, core: 2. Of those that a mesh axis runs over, the one named last changes fastest.
Arguments:
- queries: bfloat16 [32, 64, 128], P('node', 'mp'), may hold values from -8 to 8
- root_keys: bfloat16 [16384, 8, 128], P('node', 'mp'), may hold values from -6 to 6
- root_values: bfloat16 [16384, 8, 128], P('node', 'mp'), may hold values from -6 to 6
- mid_keys: bfloat16 [8, 1024, 8, 128], P('node', None, 'mp'), may hold values from -6 to 6
- mid_values: bfloat16 [8, 1024, 8, 128], P('node', None, 'mp'), may hold values from -6 to 6
- leaf_keys: bfloat16 [32, 256, 8, 128], P('node', None, 'mp'), may hold values from -6 to 6
- leaf_values: bfloat16 [32, 256, 8, 128], P('node', None, 'mp'), may hold values from -6 to 6
- mid_length: int32 [8], replicated, may hold values from 1 to 1024
- leaf_length: int32 [32], P('node'), may hold values from 1 to 256
- branch_mid: int32 [32, 1], replicated, may hold values from 0 to 7; in each aligned block of 32 rows (0 to 31, 32 to 63, ...) at most 8 rows name the same one
- residual: bfloat16 [32, 8192], P(None, 'node'), may hold values from -6 to 6
- norm_gain: float32 [8192], P('node'), may hold values from 0.5 to 1.5
- out_weight: bfloat16 [8192, 8192], P('mp', 'node'), may hold values from -0.0625 to 0.0625
- gate_weight: bfloat16 [8192, 28672], P('node', 'mp'), may hold values from -0.0625 to 0.0625
- up_weight: bfloat16 [8192, 28672], P('node', 'mp'), may hold values from -0.0625 to 0.0625
- down_weight: bfloat16 [28672, 8192], P('mp', 'node'), may hold values from -0.03125 to 0.03125
Outputs:
- layer_out: bfloat16 [32, 8192], P('mp', 'node')
Inputs may be any that keep to these rules, and one draw needn't show every extreme that they name: `branch_mid`: every inner tree node lies on the path of 1 to 8 branches, and some node on exactly 8.
All inputs are finite; a program needn't handle non-finite values.
Results may differ from a plain program's by a relative error of at most 0.015.
Values may be sent and summed in bfloat16 or wider, within the bound.
A program may use at most 128 MiB of HBM per device.

v0:
```python
import jax
import jax.numpy as jnp
from jax import lax
from jax.sharding import PartitionSpec as P

D = 8192
CAP = 8
masked_score = -1e30
norm_eps = 1e-05


def partial_scores(grouped, key_block, value_block, usable, scaling):
    scores = (
        jnp.einsum("bkgd,lkd->bkgl", grouped, key_block, preferred_element_type=jnp.float32)
        * scaling
    )
    masking = usable[:, None, None, :]
    scores = jnp.where(masking, scores, masked_score)
    highest = jnp.max(scores, axis=-1)
    weights = jnp.where(masking, jnp.exp(scores - highest[..., None]), 0.0)
    weighted = jnp.einsum(
        "bkgl,lkd->bkgd",
        weights.astype(jnp.bfloat16),
        value_block,
        preferred_element_type=jnp.float32,
    )
    return (highest, jnp.sum(weights, axis=-1), weighted)


def combine_parts(earlier, later):
    highest = jnp.maximum(earlier[0], later[0])
    first_factor = jnp.exp(earlier[0] - highest)
    second_factor = jnp.exp(later[0] - highest)
    totals = earlier[1] * first_factor + later[1] * second_factor
    weighted = earlier[2] * first_factor[..., None] + later[2] * second_factor[..., None]
    return (highest, totals, weighted)


def on_device(
    queries,
    root_keys,
    root_values,
    mid_keys,
    mid_values,
    leaf_keys,
    leaf_values,
    mid_length,
    leaf_length,
    branch_mid,
    residual,
    norm_gain,
    out_weight,
    gate_weight,
    up_weight,
    down_weight,
):
    owned = queries.shape[0]
    local_heads = queries.shape[1]
    head_size = queries.shape[2]
    local_groups = root_keys.shape[1]
    group_size = local_heads // local_groups
    scaling = head_size ** (-0.5)
    node_count = lax.axis_size("node")
    gathered = lax.all_gather(queries, "node", axis=0, tiled=True)
    every_branch = gathered.shape[0]
    grouped = gathered.reshape(every_branch, local_groups, group_size, head_size)
    root_usable = jnp.ones((every_branch, root_keys.shape[0]), dtype=bool)
    root_part = partial_scores(grouped, root_keys, root_values, root_usable, scaling)
    local_mids = mid_keys.shape[0]
    node_ids = lax.axis_index("node") * local_mids + jnp.arange(local_mids, dtype=jnp.int32)
    routing = branch_mid[:, 0]
    matching = routing[None, :] == node_ids[:, None]
    ranking = jnp.cumsum(matching.astype(jnp.int32), axis=1) - 1
    selected = matching[:, None, :] & (
        ranking[:, None, :] == jnp.arange(CAP, dtype=jnp.int32)[None, :, None]
    )
    picked = jnp.einsum(
        "ncb,bkgd->nckgd",
        selected.astype(jnp.bfloat16),
        grouped,
        preferred_element_type=jnp.float32,
    ).astype(jnp.bfloat16)
    slot_index = jnp.arange(mid_keys.shape[1])

    def node_partial(inputs):
        node_queries, node_keys, node_values, node_id = inputs
        usable = jnp.broadcast_to(
            slot_index[None, :] < mid_length[node_id], (CAP, slot_index.shape[0])
        )
        return partial_scores(node_queries, node_keys, node_values, usable, scaling)

    node_high, node_totals, node_weighted = lax.map(
        node_partial, (picked, mid_keys, mid_values, node_ids)
    )
    chosen = selected.astype(jnp.float32)
    covered = jnp.sum(chosen, axis=(0, 1))
    back_high = (
        jnp.einsum("ncb,nckg->bkg", chosen, node_high, precision=lax.Precision.HIGHEST)
        + ((1.0 - covered) * masked_score)[:, None, None]
    )
    back_totals = jnp.einsum("ncb,nckg->bkg", chosen, node_totals, precision=lax.Precision.HIGHEST)
    back_weighted = jnp.einsum(
        "ncb,nckgd->bkgd", chosen, node_weighted, precision=lax.Precision.HIGHEST
    )
    shared_part = combine_parts(root_part, (back_high, back_totals, back_weighted))
    peaks, totals, weighted = (
        lax.all_to_all(shared_part[0], "node", split_axis=0, concat_axis=0, tiled=True),
        lax.all_to_all(shared_part[1], "node", split_axis=0, concat_axis=0, tiled=True),
        lax.all_to_all(shared_part[2], "node", split_axis=0, concat_axis=0, tiled=True),
    )
    peaks = peaks.reshape(node_count, owned, local_groups, group_size)
    totals = totals.reshape(node_count, owned, local_groups, group_size)
    weighted = weighted.reshape(node_count, owned, local_groups, group_size, head_size)
    highest = jnp.max(peaks, axis=0)
    factor = jnp.exp(peaks - highest[None])
    merged = (
        highest,
        jnp.sum(totals * factor, axis=0),
        jnp.sum(weighted * factor[..., None], axis=0),
    )
    own_grouped = queries.reshape(owned, local_groups, group_size, head_size)
    leaf_scores = (
        jnp.einsum("bkgd,blkd->bkgl", own_grouped, leaf_keys, preferred_element_type=jnp.float32)
        * scaling
    )
    leaf_usable = (jnp.arange(leaf_keys.shape[1])[None, :] < leaf_length[:, None])[:, None, None, :]
    leaf_scores = jnp.where(leaf_usable, leaf_scores, masked_score)
    leaf_peak = jnp.max(leaf_scores, axis=-1)
    leaf_weights = jnp.where(leaf_usable, jnp.exp(leaf_scores - leaf_peak[..., None]), 0.0)
    leaf_weighted = jnp.einsum(
        "bkgl,blkd->bkgd",
        leaf_weights.astype(jnp.bfloat16),
        leaf_values,
        preferred_element_type=jnp.float32,
    )
    final_part = combine_parts(merged, (leaf_peak, jnp.sum(leaf_weights, axis=-1), leaf_weighted))
    attended = (
        (final_part[2] / final_part[1][..., None])
        .reshape(owned, local_heads * head_size)
        .astype(jnp.bfloat16)
    )
    projected = jnp.dot(
        lax.all_gather(attended, "node", axis=0, tiled=True),
        out_weight,
        preferred_element_type=jnp.float32,
    )
    projected = lax.psum(projected.astype(jnp.bfloat16), "mp").astype(jnp.float32)
    stream = residual.astype(jnp.float32) + projected
    squares = lax.psum(jnp.sum(stream * stream, axis=1), "node")
    normed = (stream * lax.rsqrt(squares[:, None] / D + norm_eps) * norm_gain[None, :]).astype(
        jnp.bfloat16
    )
    out_rows = every_branch // lax.axis_size("mp")
    gate, upward = (
        lax.psum(
            jnp.dot(normed, gate_weight, preferred_element_type=jnp.float32).astype(jnp.bfloat16),
            "node",
        ).astype(jnp.float32),
        lax.psum(
            jnp.dot(normed, up_weight, preferred_element_type=jnp.float32).astype(jnp.bfloat16),
            "node",
        ).astype(jnp.float32),
    )
    act = (jax.nn.silu(gate) * upward).astype(jnp.bfloat16)
    mlp_rows = lax.psum_scatter(
        jnp.dot(act, down_weight, preferred_element_type=jnp.float32).astype(jnp.bfloat16),
        "mp",
        scatter_dimension=0,
        tiled=True,
    ).astype(jnp.float32)
    stream_rows = lax.dynamic_slice_in_dim(stream, lax.axis_index("mp") * out_rows, out_rows, 0)
    return (stream_rows + mlp_rows).astype(jnp.bfloat16)


def solution(mesh):
    in_specs = (
        P("node", "mp", None),
        P("node", "mp", None),
        P("node", "mp", None),
        P("node", None, "mp", None),
        P("node", None, "mp", None),
        P("node", None, "mp", None),
        P("node", None, "mp", None),
        P(),
        P("node"),
        P(),
        P(None, "node"),
        P("node"),
        P("mp", "node"),
        P("node", "mp"),
        P("node", "mp"),
        P("mp", "node"),
    )
    out_specs = P("mp", "node")
    return jax.shard_map(
        on_device, mesh=mesh, in_specs=in_specs, out_specs=out_specs, check_vma=False
    )
```

profile of v0, /device:TPU:0, one launch (start us, length us, event | category | flops | bytes accessed | tf_op | source)
XLA Modules:
  0.0 297.3 jit_solution(1106771095615868161)
XLA Ops:
  6.5 1.3 dynamic_slice.18
  7.9 0.6 iota_compare_fusion.2
  8.5 0.7 compare_bitcast_fusion
  9.5 32.5 %all_gather.6 = bf16[32,16,128]{2,1,0:T(8,128)(2,1)S(1)} all-gather(bf16[4,16,128]{2,1,0:T(8,128)(2,1)} %param.16), channel_id=1, replica_groups=mesh['node'=8,'mp'=4] {'node'}, dimensions={0}, use_global_device_ids=true | all-gather | bytes 147456 | tf_op jit(solution)/shard_map/all_gather | solution.py:64
  42.2 1.4 fusion.79
  44.0 2.1 bitcast_reduce_fusion
  46.2 1.8 copy-done.1
  48.0 0.8 fusion.1
  49.0 0.7 copy.115
  49.7 5.5 %all-to-all-start.2 = ((f32[32,2,8]{2,1,0:T(2,128)}), f32[32,2,8]{2,1,0:T(2,128)S(1)}, u32[]{:S(2)}, u32[]{:S(2)}) async-start(f32[32,2,8]{2,1,0:T(2,128)} %copy.115), calls=%async_computation.2 | async-start | bytes 65536 | tf_op jit(solution)/shard_map/all_to_all | solution.py:108
  55.2 0.3 convolution_bitcast_fusion
  55.5 3.3 %fusion.13 = f32[32,2,8,128]{3,0,2,1:T(8,128)S(1)} fusion(f32[2,2048,32,8]{1,2,3,0:T(8,128)} %copy-done.1, f32[32,2,8]{0,2,1:T(8,128)S(1)} %get-tuple-element.48, bf16[2048,2,128,1]{2,1,0,3:T(2,128)(2,1)S(1)} %bitcast.75, f32[32,2,8]{0,2,1:T(8,128)S(1)} %subtract_exponential_fusion.2), kind=kOutput, calls=%fused_computation.16 | convolution fusion | flops 271646720 | bytes 5509120 | tf_op jit(solution)/shard_map/bkgl,lkd->bkgd/dot_general | solution.py:21
  58.8 0.3 fusion.80
  59.2 0.7 copy.104
  59.9 2.0 all-to-all-done.2
  61.8 4.2 %all-to-all-start.1 = ((f32[32,2,8]{2,1,0:T(2,128)}), f32[32,2,8]{2,1,0:T(2,128)S(1)}, u32[]{:S(2)}, u32[]{:S(2)}) async-start(f32[32,2,8]{2,1,0:T(2,128)} %copy.104), calls=%async_computation.1 | async-start | bytes 65536 | tf_op jit(solution)/shard_map/all_to_all | solution.py:107
  66.0 0.3 fusion.12
  66.3 0.8 copy.103
  67.2 5.5 %all-to-all-done.1 = f32[32,2,8]{2,1,0:T(2,128)S(1)} async-done(((f32[32,2,8]{2,1,0:T(2,128)}), f32[32,2,8]{2,1,0:T(2,128)S(1)}, u32[]{:S(2)}, u32[]{:S(2)}) %all-to-all-start.1) | async-done | bytes 2080 | tf_op jit(solution)/shard_map/all_to_all | solution.py:107
  72.7 3.4 %all-to-all-start = ((f32[32,2,8,128]{3,2,1,0:T(8,128)}), f32[32,2,8,128]{3,2,1,0:T(8,128)S(1)}, u32[]{:S(2)}, u32[]{:S(2)}) async-start(f32[32,2,8,128]{3,2,1,0:T(8,128)} %copy.103), calls=%async_computation | async-start | bytes 524288 | tf_op jit(solution)/shard_map/all_to_all | solution.py:109
  76.5 7.9 %all-to-all-done = f32[32,2,8,128]{3,2,1,0:T(8,128)S(1)} async-done(((f32[32,2,8,128]{3,2,1,0:T(8,128)}), f32[32,2,8,128]{3,2,1,0:T(8,128)S(1)}, u32[]{:S(2)}, u32[]{:S(2)}) %all-to-all-start) | async-done | bytes 262176 | tf_op jit(solution)/shard_map/all_to_all | solution.py:109
  84.8 30.6 %all-gather = bf16[8,4,2048]{2,1,0:T(4,128)(2,1)S(1)} all-gather(bf16[1,4,2048]{2,1,0:T(4,128)(2,1)S(1)} %reshape.273), channel_id=1, replica_groups=mesh['node'=8,'mp'=4] {'node'}, dimensions={0}, use_global_device_ids=true | all-gather | bytes 147456 | tf_op jit(solution)/shard_map/all_gather | solution.py:143
  115.4 3.6 %convolution_convert_fusion.3 = bf16[32,1024]{1,0:T(8,128)(2,1)} fusion(bf16[32,2048]{1,0:T(8,128)(2,1)S(1)} %reshape.274, bf16[2048,1024]{1,0:T(8,128)(2,1)} %param.28), kind=kOutput, calls=%fused_computation.20 | convolution fusion | flops 134250496 | bytes 4390912 | tf_op jit(solution)/shard_map/dot_general | solution.py:142
  119.1 30.0 %all-reduce.4.cloned.1.call-done = bf16[32,1024]{1,0:T(8,128)(2,1)} async-done(((bf16[32,1024]{1,0:T(8,128)(2,1)}), bf16[32,1024]{1,0:T(8,128)(2,1)}) %all-reduce.4.cloned.1.call-update) | async-done | bytes 65552 | tf_op jit(solution)/shard_map/psum | solution.py:147
  149.1 1.0 convert_add_fusion
  150.1 21.4 %psum.29 = f32[32]{0:T(128)S(1)} all-reduce(f32[32]{0:T(128)S(1)} %get-tuple-element.45), channel_id=1, replica_groups=mesh['node'=8,'mp'=4] {'node'}, use_global_device_ids=true, to_apply=%region_13.14 | all-reduce | flops 32 | bytes 256 | tf_op jit(solution)/shard_map/psum | solution.py:149
  171.4 8.7 %convolution_convert_fusion = bf16[32,7168]{1,0:T(8,128)(2,1)} fusion(bf16[1024,7168]{1,0:T(8,128)(2,1)} %param.30, f32[1024]{0:T(1024)S(1)} %copy-done.5, f32[32]{0:T(128)S(1)} %add_rsqrt_fusion, bf16[32,1024]{1,0:T(8,128)(2,1)} %all-reduce.4.cloned.1.call-done, bf16[32,1024]{1,0:T(8,128)(2,1)S(1)} %copy-done.2), kind=kOutput, calls=%fused_computation | convolution fusion | flops 470188032 | bytes 15274112 | tf_op jit(solution)/shard_map/dot_general | solution.py:160
  180.1 8.6 %convolution_convert_fusion.1 = bf16[32,7168]{1,0:T(8,128)(2,1)} fusion(bf16[1024,7168]{1,0:T(8,128)(2,1)} %param.29, f32[1024]{0:T(1024)S(1)} %copy-done.5, f32[32]{0:T(128)S(1)} %add_rsqrt_fusion, bf16[32,1024]{1,0:T(8,128)(2,1)S(1)} %copy-done.3, bf16[32,1024]{1,0:T(8,128)(2,1)S(1)} %copy-done.2), kind=kOutput, calls=%fused_computation.1 | convolution fusion | flops 470188032 | bytes 15274112 | tf_op jit(solution)/shard_map/dot_general | solution.py:156
  188.8 73.1 %all-reduce.6.cloned.1.call-done = (bf16[32,7168]{1,0:T(8,128)(2,1)}, bf16[32,7168]{1,0:T(8,128)(2,1)}) async-done(((bf16[32,7168]{1,0:T(8,128)(2,1)}, bf16[32,7168]{1,0:T(8,128)(2,1)}), (bf16[32,7168]{1,0:T(8,128)(2,1)}, bf16[32,7168]{1,0:T(8,128)(2,1)})) %all-reduce.6.cloned.1.call-update) | async-done | bytes 917520 | tf_op jit(solution)/shard_map/psum | solution.py:159
  261.8 8.7 %convolution_convert_fusion.2 = bf16[32,1024]{1,0:T(8,128)(2,1)} fusion(bf16[7168,1024]{1,0:T(8,128)(2,1)} %param.31, bf16[32,7168]{1,0:T(8,128)(2,1)} %get-tuple-element.23, bf16[32,7168]{1,0:T(8,128)(2,1)} %get-tuple-element.24), kind=kOutput, calls=%fused_computation.19 | convolution fusion | flops 471629824 | bytes 15663104 | tf_op jit(solution)/shard_map/dot_general | solution.py:166
  270.6 18.8 %reduce-scatter.2.cloned.1.call-done = bf16[8,1024]{1,0:T(8,128)(2,1)} async-done(((bf16[32,1024]{1,0:T(8,128)(2,1)}), bf16[8,1024]{1,0:T(8,128)(2,1)}) %reduce-scatter.2.cloned.1.call-update) | async-done | bytes 16400 | tf_op jit(solution)/shard_map/reduce_scatter | solution.py:165
  289.4 1.3 add_convert_fusion
  (53 shorter events, 2.1 us)
Async XLA Ops:
  6.5 49.0 %copy-start = (bf16[2048,2,128]{2,1,0:T(2,128)(2,1)S(1)}, bf16[2048,2,128]{2,1,0:T(2,128)(2,1)}, u32[]{:S(2)}) copy-start(bf16[2048,2,128]{2,1,0:T(2,128)(2,1)} %param.18) | copy-start | bytes 3145732
  44.0 11.1 %copy-start.9 = (s32[4]{0:T(128)S(1)}, s32[4]{0:T(128)}, u32[]{:S(2)}) copy-start(s32[4]{0:T(128)} %param.24) | copy-start | bytes 52
  44.0 11.2 %copy-start.7 = (bf16[1,1024,2,128]{3,2,1,0:T(2,128)(2,1)S(1)}, bf16[1,1024,2,128]{3,2,1,0:T(2,128)(2,1)}, u32[]{:S(2)}) copy-start(bf16[1,1024,2,128]{3,2,1,0:T(2,128)(2,1)} %param.20) | copy-start | bytes 1572868
  46.1 1.9 copy-start.1
  48.9 10.0 %copy-start.4 = (bf16[4,256,2,128]{3,2,1,0:T(2,128)(2,1)S(1)}, bf16[4,256,2,128]{3,2,1,0:T(2,128)(2,1)}, u32[]{:S(2)}) copy-start(bf16[4,256,2,128]{3,2,1,0:T(2,128)(2,1)} %param.21) | copy-start | bytes 1572868
  48.9 10.0 %copy-start.6 = (bf16[4,16,128]{2,1,0:T(8,128)(2,1)S(1)}, bf16[4,16,128]{2,1,0:T(8,128)(2,1)}, u32[]{:S(2)}) copy-start(bf16[4,16,128]{2,1,0:T(8,128)(2,1)} %param.16) | copy-start | bytes 49156
  49.7 12.1 %all-to-all-start.2 = ((f32[32,2,8]{2,1,0:T(2,128)}), f32[32,2,8]{2,1,0:T(2,128)S(1)}, u32[]{:S(2)}, u32[]{:S(2)}) async-start(f32[32,2,8]{2,1,0:T(2,128)} %copy.115), calls=%async_computation.2 | async-start | bytes 65536 | tf_op jit(solution)/shard_map/all_to_all | solution.py:108
  55.5 29.0 %copy-start.8 = (bf16[4,256,2,128]{3,2,1,0:T(2,128)(2,1)S(1)}, bf16[4,256,2,128]{3,2,1,0:T(2,128)(2,1)}, u32[]{:S(2)}) copy-start(bf16[4,256,2,128]{3,2,1,0:T(2,128)(2,1)} %param.22) | copy-start | bytes 1572868
  59.9 89.2 %copy-start.2 = (bf16[32,1024]{1,0:T(8,128)(2,1)S(1)}, bf16[32,1024]{1,0:T(8,128)(2,1)}, u32[]{:S(2)}) copy-start(bf16[32,1024]{1,0:T(8,128)(2,1)} %param.26) | copy-start | bytes 196612
  61.8 10.9 %all-to-all-start.1 = ((f32[32,2,8]{2,1,0:T(2,128)}), f32[32,2,8]{2,1,0:T(2,128)S(1)}, u32[]{:S(2)}, u32[]{:S(2)}) async-start(f32[32,2,8]{2,1,0:T(2,128)} %copy.104), calls=%async_computation.1 | async-start | bytes 65536 | tf_op jit(solution)/shard_map/all_to_all | solution.py:107
  66.0 105.4 %copy-start.5 = (f32[1024]{0:T(1024)S(1)}, f32[1024]{0:T(1024)}, u32[]{:S(2)}) copy-start(f32[1024]{0:T(1024)} %param.27) | copy-start | bytes 12292
  72.7 11.7 %all-to-all-start = ((f32[32,2,8,128]{3,2,1,0:T(8,128)}), f32[32,2,8,128]{3,2,1,0:T(8,128)S(1)}, u32[]{:S(2)}, u32[]{:S(2)}) async-start(f32[32,2,8,128]{3,2,1,0:T(8,128)} %copy.103), calls=%async_computation | async-start | bytes 524288 | tf_op jit(solution)/shard_map/all_to_all | solution.py:109
  76.1 73.0 %all-reduce.4.cloned.1.call-start = ((), (), s32[]{:S(2)}) async-start(), calls=%async_computation.4 | async-start | bytes 131072 | tf_op jit(solution)/shard_map/psum | solution.py:147
  119.0 142.8 %all-reduce.6.cloned.1.call-start = ((), (), s32[]{:S(2)}) async-start(), calls=%async_computation.6 | async-start | bytes 1835008 | tf_op jit(solution)/shard_map/psum | solution.py:159
  171.4 8.7 %copy-start.3 = (bf16[32,1024]{1,0:T(8,128)(2,1)S(1)}, bf16[32,1024]{1,0:T(8,128)(2,1)}, u32[]{:S(2)}) copy-start(bf16[32,1024]{1,0:T(8,128)(2,1)} %all-reduce.4.cloned.1.call-done) | copy-start | bytes 196612
  188.7 100.7 %reduce-scatter.2.cloned.1.call-start = ((), (), s32[]{:S(2)}) async-start(), calls=%async_computation.5 | async-start | bytes 81920 | tf_op jit(solution)/shard_map/reduce_scatter | solution.py:165
Sparse Core Ops, SparseCore 0:
  119.1 29.9 all-reduce.3
  188.9 72.9 all-reduce.5
  270.7 18.6 reduce-scatter.1
where the time goes:
time: 298 us; the launch traced here: 297 us
  waiting for transfers between devices  137 us (46%)
  blocking collectives  84.5 us (28%)
  matrix products  38 us (13%)
  between operations  13.3 us (4%)
  starting transfers between devices  13.1 us (4%)
  local copies, waits for them, and re-layouts  5.71 us (2%)
  other arithmetic  5.33 us (2%)
    psum x1, waiting for transfers between devices, on_device(): lax.psum(jnp.dot(normed, up_weight, preferred_element_type=jnp.float32).a...  73.1 us
    all_gather x1, blocking collectives, on_device(): gathered = lax.all_gather(queries, 'node', axis=0, tiled=True)  32.5 us
    all_gather x1, blocking collectives, on_device(): lax.all_gather(attended, 'node', axis=0, tiled=True)  30.6 us
    psum x1, waiting for transfers between devices, on_device(): lax.psum(projected.astype(jnp.bfloat16), 'mp').astype(jnp.float32)  30 us
    psum x1, blocking collectives, on_device(): squares = lax.psum(jnp.sum(stream * stream, axis=1), 'node')  21.4 us
    reduce_scatter x1, waiting for transfers between devices, on_device(): lax.psum_scatter(jnp.dot(act, down_weight, preferred_element_type=jnp.flo...  18.8 us
    dot_general x1, matrix products, on_device(): jnp.dot(act, down_weight, preferred_element_type=jnp.float32)  8.71 us
    dot_general x1, matrix products, on_device(): jnp.dot(normed, up_weight, preferred_element_type=jnp.float32)  8.67 us
  transfers between devices with their start and end apart: 6, of which 6 were waited for; matrix products, arithmetic and copies ran while one was open for 2% of the time, Pallas kernels for 0%

commit v1 on v0

--- a/solution.py
+++ b/solution.py
@@ -144,7 +144,9 @@
         out_weight,
         preferred_element_type=jnp.float32,
     )
-    projected = lax.psum(projected.astype(jnp.bfloat16), "mp").astype(jnp.float32)
+    projected = jnp.sum(lax.all_gather(projected.astype(jnp.bfloat16), "mp"), axis=0).astype(
+        jnp.float32
+    )
     stream = residual.astype(jnp.float32) + projected
     squares = lax.psum(jnp.sum(stream * stream, axis=1), "node")
     normed = (stream * lax.rsqrt(squares[:, None] / D + norm_eps) * norm_gain[None, :]).astype(

time: 298 us -> 271 us (0.909)
  waiting for transfers between devices: 137 us -> 108 us
  blocking collectives: 84.5 us -> 87.6 us
    psum x1 -> x0, waiting for transfers between devices: 30 us -> none  [on_device(): lax.psum(projected.astype(jnp.bfloat16), 'mp').astype(jnp.float32)]
    all_gather x0 -> x1, blocking collectives: none -> 5.77 us  [on_device(): lax.all_gather(projected.astype(jnp.bfloat16), 'mp')]
  transfers between devices with their start and end apart: 6 -> 5, of which waited for: 6 -> 5; matrix products, arithmetic and copies ran while one was open for 2% -> 2% of each run, Pallas kernels for 0% -> 0%
where the time goes in v1:
time: 271 us; the launch traced here: 270 us
  waiting for transfers between devices  108 us (40%)
  blocking collectives  87.6 us (32%)
  matrix products  37.3 us (14%)
  between operations  13.6 us (5%)
  starting transfers between devices  13 us (5%)
  local copies, waits for them, and re-layouts  5.72 us (2%)
  other arithmetic  4.53 us (2%)
    psum x1, waiting for transfers between devices, on_device(): lax.psum(jnp.dot(normed, up_weight, preferred_element_type=jnp.float32).a...  74.2 us
    all_gather x1, blocking collectives, on_device(): gathered = lax.all_gather(queries, 'node', axis=0, tiled=True)  32.5 us
    all_gather x1, blocking collectives, on_device(): lax.all_gather(attended, 'node', axis=0, tiled=True)  30.6 us
    reduce_scatter x1, waiting for transfers between devices, on_device(): lax.psum_scatter(jnp.dot(act, down_weight, preferred_element_type=jnp.flo...  18.8 us
    psum x1, blocking collectives, on_device(): squares = lax.psum(jnp.sum(stream * stream, axis=1), 'node')  18.8 us
    dot_general x1, matrix products, on_device(): jnp.dot(act, down_weight, preferred_element_type=jnp.float32)  8.71 us
    dot_general x1, matrix products, on_device(): jnp.dot(normed, gate_weight, preferred_element_type=jnp.float32)  8.62 us
    dot_general x1, matrix products, on_device(): jnp.dot(normed, up_weight, preferred_element_type=jnp.float32)  8.6 us
  transfers between devices with their start and end apart: 5, of which 5 were waited for; matrix products, arithmetic and copies ran while one was open for 2% of the time, Pallas kernels for 0%

profile of v1, /device:TPU:0, one launch (start us, length us, event | category | flops | bytes accessed | tf_op | source)
XLA Modules:
  0.0 270.1 jit_solution(3275656874343743828)
XLA Ops:
  6.5 1.3 dynamic_slice.18
  7.9 0.6 iota_compare_fusion.2
  8.5 0.7 compare_bitcast_fusion
  9.5 32.5 %all_gather.12 = bf16[32,16,128]{2,1,0:T(8,128)(2,1)S(1)} all-gather(bf16[4,16,128]{2,1,0:T(8,128)(2,1)} %param.16), channel_id=1, replica_groups=mesh['node'=8,'mp'=4] {'node'}, dimensions={0}, use_global_device_ids=true | all-gather | bytes 147456 | tf_op jit(solution)/shard_map/all_gather | solution.py:64
  42.2 1.4 fusion.79
  44.0 2.1 bitcast_reduce_fusion
  46.2 1.8 copy-done.1
  48.0 0.8 fusion.1
  49.0 0.7 copy.115
  49.7 5.5 %all-to-all-start.2 = ((f32[32,2,8]{2,1,0:T(2,128)}), f32[32,2,8]{2,1,0:T(2,128)S(1)}, u32[]{:S(2)}, u32[]{:S(2)}) async-start(f32[32,2,8]{2,1,0:T(2,128)} %copy.115), calls=%async_computation.2 | async-start | bytes 65536 | tf_op jit(solution)/shard_map/all_to_all | solution.py:108
  55.2 0.3 convolution_bitcast_fusion
  55.5 3.3 %fusion.13 = f32[32,2,8,128]{3,0,2,1:T(8,128)S(1)} fusion(f32[2,2048,32,8]{1,2,3,0:T(8,128)} %copy-done.1, f32[32,2,8]{0,2,1:T(8,128)S(1)} %get-tuple-element.48, bf16[2048,2,128,1]{2,1,0,3:T(2,128)(2,1)S(1)} %bitcast.76, f32[32,2,8]{0,2,1:T(8,128)S(1)} %subtract_exponential_fusion.2), kind=kOutput, calls=%fused_computation.16 | convolution fusion | flops 271646720 | bytes 5509120 | tf_op jit(solution)/shard_map/bkgl,lkd->bkgd/dot_general | solution.py:21
  58.8 0.3 fusion.80
  59.2 0.7 copy.104
  59.9 2.0 all-to-all-done.2
  61.8 4.0 %all-to-all-start.1 = ((f32[32,2,8]{2,1,0:T(2,128)}), f32[32,2,8]{2,1,0:T(2,128)S(1)}, u32[]{:S(2)}, u32[]{:S(2)}) async-start(f32[32,2,8]{2,1,0:T(2,128)} %copy.104), calls=%async_computation.1 | async-start | bytes 65536 | tf_op jit(solution)/shard_map/all_to_all | solution.py:107
  65.8 0.3 fusion.12
  66.2 0.8 copy.103
  67.0 5.5 %all-to-all-done.1 = f32[32,2,8]{2,1,0:T(2,128)S(1)} async-done(((f32[32,2,8]{2,1,0:T(2,128)}), f32[32,2,8]{2,1,0:T(2,128)S(1)}, u32[]{:S(2)}, u32[]{:S(2)}) %all-to-all-start.1) | async-done | bytes 2080 | tf_op jit(solution)/shard_map/all_to_all | solution.py:107
  72.5 3.4 %all-to-all-start = ((f32[32,2,8,128]{3,2,1,0:T(8,128)}), f32[32,2,8,128]{3,2,1,0:T(8,128)S(1)}, u32[]{:S(2)}, u32[]{:S(2)}) async-start(f32[32,2,8,128]{3,2,1,0:T(8,128)} %copy.103), calls=%async_computation | async-start | bytes 524288 | tf_op jit(solution)/shard_map/all_to_all | solution.py:109
  76.3 7.9 %all-to-all-done = f32[32,2,8,128]{3,2,1,0:T(8,128)S(1)} async-done(((f32[32,2,8,128]{3,2,1,0:T(8,128)}), f32[32,2,8,128]{3,2,1,0:T(8,128)S(1)}, u32[]{:S(2)}, u32[]{:S(2)}) %all-to-all-start) | async-done | bytes 262176 | tf_op jit(solution)/shard_map/all_to_all | solution.py:109
  84.4 0.2 fusion.19
  84.6 30.6 %all-gather.1 = bf16[8,4,2048]{2,1,0:T(4,128)(2,1)S(1)} all-gather(bf16[1,4,2048]{2,1,0:T(4,128)(2,1)S(1)} %reshape.274), channel_id=1, replica_groups=mesh['node'=8,'mp'=4] {'node'}, dimensions={0}, use_global_device_ids=true | all-gather | bytes 147456 | tf_op jit(solution)/shard_map/all_gather | solution.py:143
  115.2 3.0 %convolution_convert_fusion.3 = bf16[32,1024]{1,0:T(8,128)(2,1)S(1)} fusion(bf16[32,2048]{1,0:T(8,128)(2,1)S(1)} %reshape.275, bf16[2048,1024]{1,0:T(8,128)(2,1)} %param.28), kind=kOutput, calls=%fused_computation.20 | convolution fusion | flops 134250496 | bytes 4390912 | tf_op jit(solution)/shard_map/dot_general | solution.py:142
  118.2 5.8 %all-gather = bf16[128,1024]{1,0:T(8,128)(2,1)S(1)} all-gather(bf16[32,1024]{1,0:T(8,128)(2,1)S(1)} %convolution_convert_fusion.3), channel_id=2, replica_groups=mesh['node'=8,'mp'=4] {'mp'}, dimensions={0}, use_global_device_ids=true | all-gather | bytes 327680 | tf_op jit(solution)/shard_map/all_gather | solution.py:147
  124.2 18.8 %psum.21 = f32[32]{0:T(128)S(1)} all-reduce(f32[32]{0:T(128)S(1)} %get-tuple-element.45), channel_id=1, replica_groups=mesh['node'=8,'mp'=4] {'node'}, use_global_device_ids=true, to_apply=%region_13.14 | all-reduce | flops 32 | bytes 256 | tf_op jit(solution)/shard_map/psum | solution.py:151
  143.0 8.6 %convolution_convert_fusion = bf16[32,7168]{1,0:T(8,128)(2,1)} fusion(bf16[1024,7168]{1,0:T(8,128)(2,1)} %param.30, f32[1024]{0:T(1024)S(1)} %copy-done.4, f32[32]{0:T(128)S(1)} %add_rsqrt_fusion, bf16[32,1024]{1,0:T(8,128)(2,1)S(1)} %reduce_sum.82, bf16[32,1024]{1,0:T(8,128)(2,1)S(1)} %copy-done.2), kind=kOutput, calls=%fused_computation | convolution fusion | flops 470188032 | bytes 15274112 | tf_op jit(solution)/shard_map/dot_general | solution.py:162
  151.6 8.6 %convolution_convert_fusion.1 = bf16[32,7168]{1,0:T(8,128)(2,1)} fusion(bf16[1024,7168]{1,0:T(8,128)(2,1)} %param.29, f32[1024]{0:T(1024)S(1)} %copy-done.4, f32[32]{0:T(128)S(1)} %add_rsqrt_fusion, bf16[32,1024]{1,0:T(8,128)(2,1)S(1)} %reduce_sum.82, bf16[32,1024]{1,0:T(8,128)(2,1)S(1)} %copy-done.2), kind=kOutput, calls=%fused_computation.1 | convolution fusion | flops 470188032 | bytes 15274112 | tf_op jit(solution)/shard_map/dot_general | solution.py:158
  160.3 74.2 %all-reduce.3.cloned.1.call-done = (bf16[32,7168]{1,0:T(8,128)(2,1)}, bf16[32,7168]{1,0:T(8,128)(2,1)}) async-done(((bf16[32,7168]{1,0:T(8,128)(2,1)}, bf16[32,7168]{1,0:T(8,128)(2,1)}), (bf16[32,7168]{1,0:T(8,128)(2,1)}, bf16[32,7168]{1,0:T(8,128)(2,1)})) %all-reduce.3.cloned.1.call-update) | async-done | bytes 917520 | tf_op jit(solution)/shard_map/psum | solution.py:161
  234.4 8.7 %convolution_convert_fusion.2 = bf16[32,1024]{1,0:T(8,128)(2,1)} fusion(bf16[7168,1024]{1,0:T(8,128)(2,1)} %param.31, bf16[32,7168]{1,0:T(8,128)(2,1)} %get-tuple-element.23, bf16[32,7168]{1,0:T(8,128)(2,1)} %get-tuple-element.24), kind=kOutput, calls=%fused_computation.19 | convolution fusion | flops 471629824 | bytes 15663104 | tf_op jit(solution)/shard_map/dot_general | solution.py:168
  243.2 18.8 %reduce-scatter.2.cloned.1.call-done = bf16[8,1024]{1,0:T(8,128)(2,1)} async-done(((bf16[32,1024]{1,0:T(8,128)(2,1)}), bf16[8,1024]{1,0:T(8,128)(2,1)}) %reduce-scatter.2.cloned.1.call-update) | async-done | bytes 16400 | tf_op jit(solution)/shard_map/reduce_scatter | solution.py:167
  262.0 1.3 add_convert_fusion
  (50 shorter events, 1.9 us)
Async XLA Ops:
  6.5 49.0 %copy-start = (bf16[2048,2,128]{2,1,0:T(2,128)(2,1)S(1)}, bf16[2048,2,128]{2,1,0:T(2,128)(2,1)}, u32[]{:S(2)}) copy-start(bf16[2048,2,128]{2,1,0:T(2,128)(2,1)} %param.18) | copy-start | bytes 3145732
  44.0 11.1 %copy-start.8 = (s32[4]{0:T(128)S(1)}, s32[4]{0:T(128)}, u32[]{:S(2)}) copy-start(s32[4]{0:T(128)} %param.24) | copy-start | bytes 52
  44.0 11.2 %copy-start.6 = (bf16[1,1024,2,128]{3,2,1,0:T(2,128)(2,1)S(1)}, bf16[1,1024,2,128]{3,2,1,0:T(2,128)(2,1)}, u32[]{:S(2)}) copy-start(bf16[1,1024,2,128]{3,2,1,0:T(2,128)(2,1)} %param.20) | copy-start | bytes 1572868
  46.1 1.9 copy-start.1
  48.9 10.0 %copy-start.3 = (bf16[4,256,2,128]{3,2,1,0:T(2,128)(2,1)S(1)}, bf16[4,256,2,128]{3,2,1,0:T(2,128)(2,1)}, u32[]{:S(2)}) copy-start(bf16[4,256,2,128]{3,2,1,0:T(2,128)(2,1)} %param.21) | copy-start | bytes 1572868
  48.9 10.0 %copy-start.5 = (bf16[4,16,128]{2,1,0:T(8,128)(2,1)S(1)}, bf16[4,16,128]{2,1,0:T(8,128)(2,1)}, u32[]{:S(2)}) copy-start(bf16[4,16,128]{2,1,0:T(8,128)(2,1)} %param.16) | copy-start | bytes 49156
  49.7 12.1 %all-to-all-start.2 = ((f32[32,2,8]{2,1,0:T(2,128)}), f32[32,2,8]{2,1,0:T(2,128)S(1)}, u32[]{:S(2)}, u32[]{:S(2)}) async-start(f32[32,2,8]{2,1,0:T(2,128)} %copy.115), calls=%async_computation.2 | async-start | bytes 65536 | tf_op jit(solution)/shard_map/all_to_all | solution.py:108
  55.5 28.8 %copy-start.7 = (bf16[4,256,2,128]{3,2,1,0:T(2,128)(2,1)S(1)}, bf16[4,256,2,128]{3,2,1,0:T(2,128)(2,1)}, u32[]{:S(2)}) copy-start(bf16[4,256,2,128]{3,2,1,0:T(2,128)(2,1)} %param.22) | copy-start | bytes 1572868
  61.8 10.7 %all-to-all-start.1 = ((f32[32,2,8]{2,1,0:T(2,128)}), f32[32,2,8]{2,1,0:T(2,128)S(1)}, u32[]{:S(2)}, u32[]{:S(2)}) async-start(f32[32,2,8]{2,1,0:T(2,128)} %copy.104), calls=%async_computation.1 | async-start | bytes 65536 | tf_op jit(solution)/shard_map/all_to_all | solution.py:107
  66.2 57.9 %copy-start.2 = (bf16[32,1024]{1,0:T(8,128)(2,1)S(1)}, bf16[32,1024]{1,0:T(8,128)(2,1)}, u32[]{:S(2)}) copy-start(bf16[32,1024]{1,0:T(8,128)(2,1)} %param.26) | copy-start | bytes 196612
  66.2 76.8 %copy-start.4 = (f32[1024]{0:T(1024)S(1)}, f32[1024]{0:T(1024)}, u32[]{:S(2)}) copy-start(f32[1024]{0:T(1024)} %param.27) | copy-start | bytes 12292
  72.5 11.7 %all-to-all-start = ((f32[32,2,8,128]{3,2,1,0:T(8,128)}), f32[32,2,8,128]{3,2,1,0:T(8,128)S(1)}, u32[]{:S(2)}, u32[]{:S(2)}) async-start(f32[32,2,8,128]{3,2,1,0:T(8,128)} %copy.103), calls=%async_computation | async-start | bytes 524288 | tf_op jit(solution)/shard_map/all_to_all | solution.py:109
  76.0 158.5 %all-reduce.3.cloned.1.call-start = ((), (), s32[]{:S(2)}) async-start(), calls=%async_computation.5 | async-start | bytes 1835008 | tf_op jit(solution)/shard_map/psum | solution.py:161
  160.2 101.8 %reduce-scatter.2.cloned.1.call-start = ((), (), s32[]{:S(2)}) async-start(), calls=%async_computation.4 | async-start | bytes 81920 | tf_op jit(solution)/shard_map/reduce_scatter | solution.py:167
Sparse Core Ops, SparseCore 0:
  160.3 74.0 all-reduce.2
  243.3 18.6 reduce-scatter.1
